TPU v7x, 32 devices: a whole 2x2x4 slice. The times are simulated.
32 devices in a mesh: mem: 8 (over z, y), lat: 4 (over x, core).
Axes of the slice: x: 2, y: 2, z: 4, core: 2. Of those that a mesh axis runs over, the one named last changes fastest.
Arguments:
- prior_sample_states: bfloat16 [16, 2, 16, 1024], P('mem', None, 'lat'), may hold values from -6 to 6
- wind_cfl_ratios: float32 [2, 16, 1024], P(None, 'lat'), may hold values from -0.45 to 0.45
- obs_cell: int32 [4, 2048], P('lat', 'mem'), may hold values from 0 to 511
- obs_value: float32 [4, 2048], P('lat', 'mem'), may hold values from -6 to 6
- obs_precision: float32 [4, 2048], P('lat', 'mem'), may hold values from 0.25 to 4
- neighbours: int32 [16, 8, 512], P('lat', 'mem'), may hold values from 0 to 1279, as said below
- obs_counts: int32 [16, 8], P('lat', 'mem'), may hold values from 128 to 512, as said below
Outputs:
- analysis: bfloat16 [16, 2, 16, 1024], P('mem', None, 'lat')
Inputs may be any that keep to these rules, and one draw needn't show every extreme that they name: `obs_counts`: in every tile some block's list has all 512 slots live. `neighbours`: the 512 entries of one list are distinct and index the extended set of its tile.
All inputs are finite; a program needn't handle non-finite values. Where the computation divides by a largest or mean magnitude, that divisor is 1e-20 or more.
Results may differ from a plain program's by a relative error of at most 0.0053.
Values may be sent and summed in bfloat16 or wider, within the bound.
A program may use at most 64 MiB of HBM per device.

v0:
```python
import jax
import jax.numpy as jnp
from jax import lax
from jax.sharding import PartitionSpec as P

PATCH_WIDTH = 128
SECTIONS = 4
NS_ITERS = 6
LOC_ROWS = 2
LOC_COLS = 64


KAPPA = (0.025, 0.0125)
HIGHEST = lax.Precision.HIGHEST


def with_halo(cells, sides, width):
    for axis, dim in sides:
        count = lax.axis_size(axis)
        ends = count - 1
        head = lax.slice_in_dim(cells, 0, width, axis=dim)
        tail = lax.slice_in_dim(cells, cells.shape[dim] - width, cells.shape[dim], axis=dim)
        cells = jnp.concatenate(
            [
                lax.ppermute(tail, axis, [(i, (i + 1) % count) for i in range(ends)]),
                cells,
                lax.ppermute(head, axis, [((i + 1) % count, i) for i in range(ends)]),
            ],
            axis=dim,
        )
    return cells


def advance(padded, east_wind, north_wind, diffusion):
    centre = padded[:, 1:-1, :]
    north_row = padded[:, 2:, :]
    south_row = padded[:, :-2, :]
    widened = jnp.pad(centre, ((0, 0), (0, 0), (1, 1)))
    west_cell = widened[:, :, :-2]
    east_cell = widened[:, :, 2:]
    transport = (
        jnp.maximum(east_wind, 0.0) * (centre - west_cell)
        + jnp.minimum(east_wind, 0.0) * (east_cell - centre)
        + jnp.maximum(north_wind, 0.0) * (centre - south_row)
        + jnp.minimum(north_wind, 0.0) * (north_row - centre)
    )
    return (
        centre
        - transport
        + diffusion * (north_row + south_row + east_cell + west_cell - 4.0 * centre)
    )


def place_piece(piece, sample_realizations, row_shift, col_shift):
    return jnp.concatenate(
        [
            piece[: sample_realizations + 2],
            piece[sample_realizations + 2 : sample_realizations + 3] + row_shift,
            piece[sample_realizations + 3 :] + col_shift,
        ],
        axis=0,
    )


def analyze(mesh_patch, extended, block_lists, block_counts):
    sample_realizations = mesh_patch.shape[0]
    analysis_block_count = mesh_patch.shape[2]
    tile_width = mesh_patch.shape[3]
    extent = extended.shape[1]
    slot_count = block_lists.shape[1]
    obs_ens = extended[:sample_realizations]
    obs_mean = jnp.mean(obs_ens, axis=0)
    spread = obs_ens - obs_mean
    innovation = extended[sample_realizations] - obs_mean
    precision = extended[sample_realizations + 1]
    obs_row = extended[sample_realizations + 2]
    obs_col = extended[sample_realizations + 3]
    active = (jnp.arange(slot_count, dtype=jnp.int32)[None, :] < block_counts[:, None]).astype(
        jnp.float32
    )
    block_ids = jnp.broadcast_to(
        jnp.arange(analysis_block_count, dtype=jnp.int32)[:, None], block_lists.shape
    )
    membership = (
        jnp.zeros((analysis_block_count, extent), jnp.float32)
        .at[block_ids, block_lists]
        .set(active)
    )
    block_row = jnp.arange(analysis_block_count, dtype=jnp.float32)[:, None]
    row_gap = obs_row[None, :] - block_row
    col_gap = obs_col[None, :] - 0.5 * (tile_width - 1)
    tapering = jnp.exp(-0.5 * ((row_gap / LOC_ROWS) ** 2 + (col_gap / LOC_COLS) ** 2))
    weight = membership * tapering * precision[None, :]
    weighted = spread[None, :, :] * weight[:, None, :]
    gram_matrix = jnp.einsum("rek,fk->ref", weighted, spread, precision=HIGHEST)
    forcing = jnp.einsum("ek,rk->re", spread, weight * innovation[None, :], precision=HIGHEST)
    identity = jnp.eye(sample_realizations, dtype=jnp.float32)
    system = (sample_realizations - 1.0) * identity + gram_matrix
    bounds = sample_realizations - 1.0 + jnp.max(jnp.sum(jnp.abs(gram_matrix), axis=2), axis=1)
    upper_iter = system / bounds[:, None, None]
    lower_iter = jnp.broadcast_to(identity, system.shape)
    for iteration in range(NS_ITERS):
        factor = 1.5 * identity - 0.5 * jnp.einsum(
            "rij,rjk->rik", lower_iter, upper_iter, precision=HIGHEST
        )
        upper_iter = jnp.einsum("rij,rjk->rik", upper_iter, factor, precision=HIGHEST)
        lower_iter = jnp.einsum("rij,rjk->rik", factor, lower_iter, precision=HIGHEST)
    inv_root = lower_iter / jnp.sqrt(bounds)[:, None, None]
    half_shift = jnp.einsum("rij,rj->ri", inv_root, forcing, precision=HIGHEST)
    mean_shift = jnp.einsum("rij,rj->ri", inv_root, half_shift, precision=HIGHEST)
    weights = jnp.sqrt(sample_realizations - 1.0) * inv_root + mean_shift[:, :, None]
    fields = mesh_patch.astype(jnp.float32)
    centre = jnp.mean(fields, axis=0)
    anomalies = fields - centre
    updated = centre + jnp.einsum("kvrc,rkm->mvrc", anomalies, weights, precision=HIGHEST)
    return updated.astype(jnp.bfloat16)


def on_device(
    prior_sample_states, wind_cfl_ratios, obs_cell, obs_value, obs_precision, neighbours, obs_counts
):
    ensemble_count = prior_sample_states.shape[0]
    analysis_block_count = prior_sample_states.shape[2]
    longitude_index = prior_sample_states.shape[3]
    present_states = prior_sample_states.astype(jnp.float32).reshape(
        ensemble_count * 2, analysis_block_count, longitude_index
    )
    diffusion = jnp.tile(jnp.array(KAPPA, jnp.float32).reshape(2, 1, 1), (ensemble_count, 1, 1))
    for section_index in range(SECTIONS):
        padded = with_halo(present_states, (("lat", 1),), 1)
        present_states = advance(padded, wind_cfl_ratios[0], wind_cfl_ratios[1], diffusion)
    predict_advance = present_states.astype(jnp.bfloat16).reshape(
        ensemble_count, 2, analysis_block_count, longitude_index
    )
    cells = obs_cell[0]
    own_meta = jnp.stack(
        [
            obs_value[0],
            obs_precision[0],
            (cells // PATCH_WIDTH).astype(jnp.float32),
            (cells % PATCH_WIDTH).astype(jnp.float32),
        ],
        axis=0,
    )
    mesh_patches = lax.all_to_all(predict_advance, "mem", split_axis=3, concat_axis=0, tiled=True)
    sample_realizations = mesh_patches.shape[0]
    own_obs = jnp.take(mesh_patches[:, 0].reshape(sample_realizations, -1), cells, axis=1).astype(
        jnp.float32
    )
    combined = jnp.concatenate([own_obs, own_meta], axis=0)
    beside_all = with_halo(combined[None, None], (("mem", 1), ("lat", 0)), 1)
    pieces = [
        beside_all[1, 1],
        beside_all[0, 1],
        beside_all[2, 1],
        beside_all[1, 0],
        beside_all[1, 2],
    ]
    row_span = float(analysis_block_count)
    col_span = float(PATCH_WIDTH)
    shifts = [(0.0, 0.0), (-row_span, 0.0), (row_span, 0.0), (0.0, -col_span), (0.0, col_span)]
    extended = jnp.concatenate(
        [
            place_piece(pieces[slot], sample_realizations, shifts[slot][0], shifts[slot][1])
            for slot in range(5)
        ],
        axis=1,
    )
    updated = analyze(mesh_patches, extended, neighbours[:, 0, :], obs_counts[:, 0])
    return lax.all_to_all(updated, "mem", split_axis=0, concat_axis=3, tiled=True)


def solution(mesh):
    placed = (
        P("mem", None, "lat", None),
        P(None, "lat", None),
        P("lat", "mem"),
        P("lat", "mem"),
        P("lat", "mem"),
        P("lat", "mem", None),
        P("lat", "mem"),
    )
    return jax.shard_map(
        on_device,
        mesh=mesh,
        in_specs=placed,
        out_specs=P("mem", None, "lat", None),
        check_vma=False,
    )
```

profile of v0, /device:TPU:0, one launch (start us, length us, event | category | flops | bytes accessed | tf_op | source)
XLA Modules:
  0.0 92.3 jit_solution(944328057822813094)
XLA Ops:
  0.0 0.8 bitcast_convert_fusion
  0.8 2.4 %collective-permute-start = (f32[4,1,1024]{2,0,1:T(4,128)S(1)}, f32[4,1,1024]{2,0,1:T(4,128)S(1)}, u32[]{:S(2)}, u32[]{:S(2)}) collective-permute-start(f32[4,1,1024]{2,0,1:T(4,128)S(1)} %get-tuple-element.17), channel_id=1, source_target_pairs={{0,1},{1,2},{2,3},{4,5},{5,6},{6,7},{8,9},{9,10},{10,11},{12,13},{... | collective-permute-start | bytes 49160 | tf_op jit(solution)/shard_map/ppermute | solution.py:25
  3.2 1.3 %collective-permute-start.1 = (f32[4,1,1024]{2,0,1:T(4,128)S(1)}, f32[4,1,1024]{2,0,1:T(4,128)S(1)}, u32[]{:S(2)}, u32[]{:S(2)}) collective-permute-start(f32[4,1,1024]{2,0,1:T(4,128)S(1)} %get-tuple-element.18), channel_id=1, source_target_pairs={{1,0},{2,1},{3,2},{5,4},{6,5},{7,6},{9,8},{10,9},{11,10},{13,12},{... | collective-permute-start | bytes 49160 | tf_op jit(solution)/shard_map/ppermute | solution.py:27
  4.6 0.6 copy-done.2
  5.3 0.6 copy-done.6
  6.0 0.6 copy-done.7
  6.7 0.6 copy-done.5
  7.4 0.6 copy-done.8
  8.2 0.2 collective-permute-done.1
  8.6 4.9 %collective-permute-start.2 = (f32[4,1,1024]{2,0,1:T(4,128)S(1)}, f32[4,1,1024]{2,0,1:T(4,128)S(1)}, u32[]{:S(2)}, u32[]{:S(2)}) collective-permute-start(f32[4,1,1024]{2,0,1:T(4,128)S(1)} %get-tuple-element.15), channel_id=1, source_target_pairs={{0,1},{1,2},{2,3},{4,5},{5,6},{6,7},{8,9},{9,10},{10,11},{12,13},{... | collective-permute-start | bytes 49160 | tf_op jit(solution)/shard_map/ppermute | solution.py:25
  13.5 1.3 %collective-permute-start.3 = (f32[4,1,1024]{2,0,1:T(4,128)S(1)}, f32[4,1,1024]{2,0,1:T(4,128)S(1)}, u32[]{:S(2)}, u32[]{:S(2)}) collective-permute-start(f32[4,1,1024]{2,0,1:T(4,128)S(1)} %get-tuple-element.16), channel_id=1, source_target_pairs={{1,0},{2,1},{3,2},{5,4},{6,5},{7,6},{9,8},{10,9},{11,10},{13,12},{... | collective-permute-start | bytes 49160 | tf_op jit(solution)/shard_map/ppermute | solution.py:27
  14.8 3.0 %collective-permute-done.3 = f32[4,1,1024]{2,0,1:T(4,128)S(1)} collective-permute-done((f32[4,1,1024]{2,0,1:T(4,128)S(1)}, f32[4,1,1024]{2,0,1:T(4,128)S(1)}, u32[]{:S(2)}, u32[]{:S(2)}) %collective-permute-start.3) | collective-permute-done | bytes 16416 | tf_op jit(solution)/shard_map/ppermute | solution.py:27
  18.0 4.4 %collective-permute-start.4 = (f32[4,1,1024]{2,0,1:T(4,128)S(1)}, f32[4,1,1024]{2,0,1:T(4,128)S(1)}, u32[]{:S(2)}, u32[]{:S(2)}) collective-permute-start(f32[4,1,1024]{2,0,1:T(4,128)S(1)} %get-tuple-element.13), channel_id=1, source_target_pairs={{0,1},{1,2},{2,3},{4,5},{5,6},{6,7},{8,9},{9,10},{10,11},{12,13},{... | collective-permute-start | bytes 49160 | tf_op jit(solution)/shard_map/ppermute | solution.py:25
  22.4 1.3 %collective-permute-start.5 = (f32[4,1,1024]{2,0,1:T(4,128)S(1)}, f32[4,1,1024]{2,0,1:T(4,128)S(1)}, u32[]{:S(2)}, u32[]{:S(2)}) collective-permute-start(f32[4,1,1024]{2,0,1:T(4,128)S(1)} %get-tuple-element.14), channel_id=1, source_target_pairs={{1,0},{2,1},{3,2},{5,4},{6,5},{7,6},{9,8},{10,9},{11,10},{13,12},{... | collective-permute-start | bytes 49160 | tf_op jit(solution)/shard_map/ppermute | solution.py:27
  23.7 1.8 %collective-permute-done.5 = f32[4,1,1024]{2,0,1:T(4,128)S(1)} collective-permute-done((f32[4,1,1024]{2,0,1:T(4,128)S(1)}, f32[4,1,1024]{2,0,1:T(4,128)S(1)}, u32[]{:S(2)}, u32[]{:S(2)}) %collective-permute-start.5) | collective-permute-done | bytes 16416 | tf_op jit(solution)/shard_map/ppermute | solution.py:27
  25.6 3.9 %collective-permute-start.6 = (f32[4,1,1024]{2,0,1:T(4,128)S(1)}, f32[4,1,1024]{2,0,1:T(4,128)S(1)}, u32[]{:S(2)}, u32[]{:S(2)}) collective-permute-start(f32[4,1,1024]{2,0,1:T(4,128)S(1)} %get-tuple-element.11), channel_id=1, source_target_pairs={{0,1},{1,2},{2,3},{4,5},{5,6},{6,7},{8,9},{9,10},{10,11},{12,13},{... | collective-permute-start | bytes 49160 | tf_op jit(solution)/shard_map/ppermute | solution.py:25
  29.5 1.3 %collective-permute-start.7 = (f32[4,1,1024]{2,0,1:T(4,128)S(1)}, f32[4,1,1024]{2,0,1:T(4,128)S(1)}, u32[]{:S(2)}, u32[]{:S(2)}) collective-permute-start(f32[4,1,1024]{2,0,1:T(4,128)S(1)} %get-tuple-element.12), channel_id=1, source_target_pairs={{1,0},{2,1},{3,2},{5,4},{6,5},{7,6},{9,8},{10,9},{11,10},{13,12},{... | collective-permute-start | bytes 49160 | tf_op jit(solution)/shard_map/ppermute | solution.py:27
  30.9 8.1 %scatter_custom_fusion = f32[5120]{0:T(1024)S(1)} fusion(s32[2048]{0:T(1024)S(1)} %bitcast.143, f32[2048]{0:T(1024)S(1)} %bitcast.144, f32[]{:T(128)} %constant.37.clone.1), kind=kCustom, calls=%fused_computation.134 | custom fusion | bytes 20484
  39.3 0.8 copy.122
  40.0 2.6 %reshape.227 = bf16[8,2,1024]{2,1,0:T(2,128)(2,1)} reshape(bf16[1024,2,2,4]{3,2,1,0:T(2,128)(2,1)S(1)} %bitcast.128) | data formatting | bytes 65536
  42.6 5.8 %all-to-all-start = ((bf16[8,2,1024]{2,1,0:T(2,128)(2,1)}), bf16[8,2,1024]{2,1,0:T(2,128)(2,1)S(1)}, u32[]{:S(2)}, u32[]{:S(2)}) async-start(bf16[8,2,1024]{2,1,0:T(2,128)(2,1)} %reshape.227), calls=%async_computation | async-start | bytes 65536 | tf_op jit(solution)/shard_map/all_to_all | solution.py:145
  48.5 6.8 %all-to-all-done = bf16[8,2,1024]{2,1,0:T(2,128)(2,1)S(1)} async-done(((bf16[8,2,1024]{2,1,0:T(2,128)(2,1)}), bf16[8,2,1024]{2,1,0:T(2,128)(2,1)S(1)}, u32[]{:S(2)}, u32[]{:S(2)}) %all-to-all-start) | async-done | bytes 32800 | tf_op jit(solution)/shard_map/all_to_all | solution.py:145
  55.3 2.2 %reshape.228 = bf16[1024,2,2,4]{3,2,1,0:T(2,128)(2,1)S(1)} reshape(bf16[8,2,1024]{2,1,0:T(2,128)(2,1)S(1)} %all-to-all-done) | data formatting | bytes 65536
  57.5 1.3 %copy.123 = bf16[2,2,4,8,128]{4,3,2,1,0:T(8,128)(2,1)S(1)} copy(bf16[2,2,4,8,128]{2,1,0,4,3:T(2,128)(2,1)S(1)} %bitcast.129) | data formatting | bytes 65536 | tf_op jit(solution)/shard_map/all_to_all | solution.py:145
  59.0 0.9 gather_fusion
  60.0 0.6 copy-done.4
  60.8 2.4 %collective-permute-start.8 = (f32[1,1,20,256]{3,2,1,0:T(8,128)S(1)}, f32[1,1,20,256]{3,2,1,0:T(8,128)S(1)}, u32[]{:S(2)}, u32[]{:S(2)}) collective-permute-start(f32[1,1,20,256]{3,2,1,0:T(8,128)S(1)} %bitcast.132), channel_id=1, source_target_pairs={{0,4},{4,8},{8,12},{12,16},{16,20},{20,24},{24,28},{1,5},{5,9},{9,... | collective-permute-start | bytes 61448 | tf_op jit(solution)/shard_map/ppermute | solution.py:25
  63.1 1.3 %collective-permute-start.9 = (f32[1,1,20,256]{3,2,1,0:T(8,128)S(1)}, f32[1,1,20,256]{3,2,1,0:T(8,128)S(1)}, u32[]{:S(2)}, u32[]{:S(2)}) collective-permute-start(f32[1,1,20,256]{3,2,1,0:T(8,128)S(1)} %bitcast.133), channel_id=1, source_target_pairs={{4,0},{8,4},{12,8},{16,12},{20,16},{24,20},{28,24},{5,1},{9,5},{13... | collective-permute-start | bytes 61448 | tf_op jit(solution)/shard_map/ppermute | solution.py:27
  64.7 4.2 %collective-permute-done.9 = f32[1,1,20,256]{3,2,1,0:T(8,128)S(1)} collective-permute-done((f32[1,1,20,256]{3,2,1,0:T(8,128)S(1)}, f32[1,1,20,256]{3,2,1,0:T(8,128)S(1)}, u32[]{:S(2)}, u32[]{:S(2)}) %collective-permute-start.9) | collective-permute-done | bytes 20512 | tf_op jit(solution)/shard_map/ppermute | solution.py:27
  68.9 1.3 %collective-permute-start.10 = (f32[1,3,20,256]{3,0,2,1:T(1,128)S(1)}, f32[1,3,20,256]{3,0,2,1:T(1,128)S(1)}, u32[]{:S(2)}, u32[]{:S(2)}) collective-permute-start(f32[1,3,20,256]{3,0,2,1:T(1,128)S(1)} %copy_dynamic-update-slice_fusion), channel_id=1, source_target_pairs={{0,1},{1,2},{2,3},{4,5},{5,6},{6,7},{8,9},{9,10},{10,11},{12,13},{... | collective-permute-start | bytes 184328 | tf_op jit(solution)/shard_map/ppermute | solution.py:25
  70.2 1.3 %collective-permute-start.11 = (f32[1,3,20,256]{3,0,2,1:T(1,128)S(1)}, f32[1,3,20,256]{3,0,2,1:T(1,128)S(1)}, u32[]{:S(2)}, u32[]{:S(2)}) collective-permute-start(f32[1,3,20,256]{3,0,2,1:T(1,128)S(1)} %copy_dynamic-update-slice_fusion), channel_id=1, source_target_pairs={{1,0},{2,1},{3,2},{5,4},{6,5},{7,6},{9,8},{10,9},{11,10},{13,12},{... | collective-permute-start | bytes 184328 | tf_op jit(solution)/shard_map/ppermute | solution.py:27
  71.6 4.1 %collective-permute-done.11 = f32[1,3,20,256]{3,0,2,1:T(1,128)S(1)} collective-permute-done((f32[1,3,20,256]{3,0,2,1:T(1,128)S(1)}, f32[1,3,20,256]{3,0,2,1:T(1,128)S(1)}, u32[]{:S(2)}, u32[]{:S(2)}) %collective-permute-start.11) | collective-permute-done | bytes 61472 | tf_op jit(solution)/shard_map/ppermute | solution.py:27
  76.0 1.3 %abs_reduce_fusion = (f32[4,16]{1,0:T(4,128)S(1)}, f32[4,16,16]{1,2,0:T(8,128)S(1)}) fusion(f32[16,1280]{1,0:T(8,128)S(1)} %slice_subtract_fusion, f32[4,1280]{1,0:T(4,128)S(1)} %multiply_multiply_fusion), kind=kOutput, calls=%fused_computation.104 | convolution fusion | flops 15812544 | bytes 106752 | tf_op jit(solution)/shard_map/rek,fk->ref/dot_general | solution.py:95
  77.4 0.3 fusion.7
  77.6 0.3 fusion.97
  78.1 0.2 fusion.6
  78.3 0.2 fusion.103
  78.6 0.2 fusion.5
  79.1 0.2 fusion.4
  79.7 0.2 fusion.3
  80.2 0.2 fusion.72
  80.3 0.2 fusion.2
  80.6 0.2 convolution_divide_fusion
  80.7 0.2 convolution_bitcast_fusion.1
  80.9 0.2 fusion.110
  81.1 0.3 fusion.1
  81.5 10.2 %all_to_all.36 = bf16[16,2,4,128]{3,1,2,0:T(2,128)(2,1)S(1)} all-to-all(bf16[16,2,4,128]{3,1,2,0:T(2,128)(2,1)S(1)} %copy.112), channel_id=1, replica_groups=mesh['mem'=8,'lat'=4] {'mem'}, dimensions={0} | all-to-all | bytes 65536 | tf_op jit(solution)/shard_map/all_to_all | solution.py:170
  91.7 0.6 all_to_all.33
  (94 shorter events, 3.7 us)
Async XLA Ops:
  0.8 3.7 %copy-start = (f32[2,4,1024]{2,1,0:T(4,128)S(1)}, f32[2,4,1024]{2,1,0:T(4,128)}, u32[]{:S(2)}) copy-start(f32[2,4,1024]{2,1,0:T(4,128)} %param.9) | copy-start | bytes 98308
  0.8 3.7 %copy-start.1 = (s32[1,256]{1,0:T(1,128)S(1)}, s32[1,256]{1,0:T(1,128)}, u32[]{:S(2)}) copy-start(s32[1,256]{1,0:T(1,128)} %param.10) | copy-start | bytes 3076
  0.8 7.3 %collective-permute-start = (f32[4,1,1024]{2,0,1:T(4,128)S(1)}, f32[4,1,1024]{2,0,1:T(4,128)S(1)}, u32[]{:S(2)}, u32[]{:S(2)}) collective-permute-start(f32[4,1,1024]{2,0,1:T(4,128)S(1)} %get-tuple-element.17), channel_id=1, source_target_pairs={{0,1},{1,2},{2,3},{4,5},{5,6},{6,7},{8,9},{9,10},{10,11},{12,13},{... | collective-permute-start | bytes 49160 | tf_op jit(solution)/shard_map/ppermute | solution.py:25
  3.2 5.2 %collective-permute-start.1 = (f32[4,1,1024]{2,0,1:T(4,128)S(1)}, f32[4,1,1024]{2,0,1:T(4,128)S(1)}, u32[]{:S(2)}, u32[]{:S(2)}) collective-permute-start(f32[4,1,1024]{2,0,1:T(4,128)S(1)} %get-tuple-element.18), channel_id=1, source_target_pairs={{1,0},{2,1},{3,2},{5,4},{6,5},{7,6},{9,8},{10,9},{11,10},{13,12},{... | collective-permute-start | bytes 49160 | tf_op jit(solution)/shard_map/ppermute | solution.py:27
  4.6 0.7 copy-start.2
  5.3 0.7 copy-start.6
  5.9 0.7 copy-start.7
  6.7 0.7 copy-start.5
  7.4 0.7 copy-start.8
  8.6 6.2 %collective-permute-start.2 = (f32[4,1,1024]{2,0,1:T(4,128)S(1)}, f32[4,1,1024]{2,0,1:T(4,128)S(1)}, u32[]{:S(2)}, u32[]{:S(2)}) collective-permute-start(f32[4,1,1024]{2,0,1:T(4,128)S(1)} %get-tuple-element.15), channel_id=1, source_target_pairs={{0,1},{1,2},{2,3},{4,5},{5,6},{6,7},{8,9},{9,10},{10,11},{12,13},{... | collective-permute-start | bytes 49160 | tf_op jit(solution)/shard_map/ppermute | solution.py:25
  13.5 4.3 %collective-permute-start.3 = (f32[4,1,1024]{2,0,1:T(4,128)S(1)}, f32[4,1,1024]{2,0,1:T(4,128)S(1)}, u32[]{:S(2)}, u32[]{:S(2)}) collective-permute-start(f32[4,1,1024]{2,0,1:T(4,128)S(1)} %get-tuple-element.16), channel_id=1, source_target_pairs={{1,0},{2,1},{3,2},{5,4},{6,5},{7,6},{9,8},{10,9},{11,10},{13,12},{... | collective-permute-start | bytes 49160 | tf_op jit(solution)/shard_map/ppermute | solution.py:27
  18.0 5.7 %collective-permute-start.4 = (f32[4,1,1024]{2,0,1:T(4,128)S(1)}, f32[4,1,1024]{2,0,1:T(4,128)S(1)}, u32[]{:S(2)}, u32[]{:S(2)}) collective-permute-start(f32[4,1,1024]{2,0,1:T(4,128)S(1)} %get-tuple-element.13), channel_id=1, source_target_pairs={{0,1},{1,2},{2,3},{4,5},{5,6},{6,7},{8,9},{9,10},{10,11},{12,13},{... | collective-permute-start | bytes 49160 | tf_op jit(solution)/shard_map/ppermute | solution.py:25
  22.4 3.1 %collective-permute-start.5 = (f32[4,1,1024]{2,0,1:T(4,128)S(1)}, f32[4,1,1024]{2,0,1:T(4,128)S(1)}, u32[]{:S(2)}, u32[]{:S(2)}) collective-permute-start(f32[4,1,1024]{2,0,1:T(4,128)S(1)} %get-tuple-element.14), channel_id=1, source_target_pairs={{1,0},{2,1},{3,2},{5,4},{6,5},{7,6},{9,8},{10,9},{11,10},{13,12},{... | collective-permute-start | bytes 49160 | tf_op jit(solution)/shard_map/ppermute | solution.py:27
  25.6 13.5 %collective-permute-start.6 = (f32[4,1,1024]{2,0,1:T(4,128)S(1)}, f32[4,1,1024]{2,0,1:T(4,128)S(1)}, u32[]{:S(2)}, u32[]{:S(2)}) collective-permute-start(f32[4,1,1024]{2,0,1:T(4,128)S(1)} %get-tuple-element.11), channel_id=1, source_target_pairs={{0,1},{1,2},{2,3},{4,5},{5,6},{6,7},{8,9},{9,10},{10,11},{12,13},{... | collective-permute-start | bytes 49160 | tf_op jit(solution)/shard_map/ppermute | solution.py:25
  29.5 9.6 %collective-permute-start.7 = (f32[4,1,1024]{2,0,1:T(4,128)S(1)}, f32[4,1,1024]{2,0,1:T(4,128)S(1)}, u32[]{:S(2)}, u32[]{:S(2)}) collective-permute-start(f32[4,1,1024]{2,0,1:T(4,128)S(1)} %get-tuple-element.12), channel_id=1, source_target_pairs={{1,0},{2,1},{3,2},{5,4},{6,5},{7,6},{9,8},{10,9},{11,10},{13,12},{... | collective-permute-start | bytes 49160 | tf_op jit(solution)/shard_map/ppermute | solution.py:27
  42.6 12.7 %all-to-all-start = ((bf16[8,2,1024]{2,1,0:T(2,128)(2,1)}), bf16[8,2,1024]{2,1,0:T(2,128)(2,1)S(1)}, u32[]{:S(2)}, u32[]{:S(2)}) async-start(bf16[8,2,1024]{2,1,0:T(2,128)(2,1)} %reshape.227), calls=%async_computation | async-start | bytes 65536 | tf_op jit(solution)/shard_map/all_to_all | solution.py:145
  60.0 0.7 copy-start.4
  60.0 0.7 copy-start.3
  60.8 3.9 %collective-permute-start.8 = (f32[1,1,20,256]{3,2,1,0:T(8,128)S(1)}, f32[1,1,20,256]{3,2,1,0:T(8,128)S(1)}, u32[]{:S(2)}, u32[]{:S(2)}) collective-permute-start(f32[1,1,20,256]{3,2,1,0:T(8,128)S(1)} %bitcast.132), channel_id=1, source_target_pairs={{0,4},{4,8},{8,12},{12,16},{16,20},{20,24},{24,28},{1,5},{5,9},{9,... | collective-permute-start | bytes 61448 | tf_op jit(solution)/shard_map/ppermute | solution.py:25
  63.1 5.7 %collective-permute-start.9 = (f32[1,1,20,256]{3,2,1,0:T(8,128)S(1)}, f32[1,1,20,256]{3,2,1,0:T(8,128)S(1)}, u32[]{:S(2)}, u32[]{:S(2)}) collective-permute-start(f32[1,1,20,256]{3,2,1,0:T(8,128)S(1)} %bitcast.133), channel_id=1, source_target_pairs={{4,0},{8,4},{12,8},{16,12},{20,16},{24,20},{28,24},{5,1},{9,5},{13... | collective-permute-start | bytes 61448 | tf_op jit(solution)/shard_map/ppermute | solution.py:27
  68.9 2.7 %collective-permute-start.10 = (f32[1,3,20,256]{3,0,2,1:T(1,128)S(1)}, f32[1,3,20,256]{3,0,2,1:T(1,128)S(1)}, u32[]{:S(2)}, u32[]{:S(2)}) collective-permute-start(f32[1,3,20,256]{3,0,2,1:T(1,128)S(1)} %copy_dynamic-update-slice_fusion), channel_id=1, source_target_pairs={{0,1},{1,2},{2,3},{4,5},{5,6},{6,7},{8,9},{9,10},{10,11},{12,13},{... | collective-permute-start | bytes 184328 | tf_op jit(solution)/shard_map/ppermute | solution.py:25
  70.2 5.5 %collective-permute-start.11 = (f32[1,3,20,256]{3,0,2,1:T(1,128)S(1)}, f32[1,3,20,256]{3,0,2,1:T(1,128)S(1)}, u32[]{:S(2)}, u32[]{:S(2)}) collective-permute-start(f32[1,3,20,256]{3,0,2,1:T(1,128)S(1)} %copy_dynamic-update-slice_fusion), channel_id=1, source_target_pairs={{1,0},{2,1},{3,2},{5,4},{6,5},{7,6},{9,8},{10,9},{11,10},{13,12},{... | collective-permute-start | bytes 184328 | tf_op jit(solution)/shard_map/ppermute | solution.py:27
where the time goes:
time: 94 us; the launch traced here: 92.3 us
  starting transfers between devices  32.8 us (35%)
  local copies, waits for them, and re-layouts  21 us (22%)
  waiting for transfers between devices  20.2 us (21%)
  blocking collectives  10.2 us (11%)
  matrix products  5.19 us (6%)
  other arithmetic  2.15 us (2%)
    ppermute x6, starting transfers between devices, with_halo(): lax.ppermute(tail, axis, [(i, (i + 1) % count) for i in range(ends)])  19.2 us
    unnamed x28, local copies, waits for them, and re-layouts  16.8 us
    ppermute x6, waiting for transfers between devices, with_halo(): lax.ppermute(head, axis, [((i + 1) % count, i) for i in range(ends)])  13.3 us
    all_to_all x1, blocking collectives, on_device(): lax.all_to_all(updated, 'mem', split_axis=0, concat_axis=3, tiled=True)  10.2 us
    ppermute x6, starting transfers between devices, with_halo(): lax.ppermute(head, axis, [((i + 1) % count, i) for i in range(ends)])  7.75 us
    all_to_all x1, waiting for transfers between devices, on_device(): lax.all_to_all(predict_advance, 'mem', split_axis=3, concat_axis=0, tiled...  6.82 us
    all_to_all x1, starting transfers between devices, on_device(): lax.all_to_all(predict_advance, 'mem', split_axis=3, concat_axis=0, tiled...  5.83 us
  transfers between devices with their start and end apart: 13, of which 7 were waited for; matrix products, arithmetic and copies ran while one was open for 10% of the time, Pallas kernels for 0%

commit v1 on v0

v1 whole, which is shorter than its diff:
```python
import functools
import math

import jax
import jax.numpy as jnp
from jax import lax
from jax.experimental import pallas as pl
from jax.experimental.pallas import tpu as pltpu
from jax.sharding import PartitionSpec as P

W = 128
SECTIONS = 4
NS_ITERS = 6
LOC_ROWS = 2
LOC_COLS = 64
KAPPA = (0.025, 0.0125)
HIGHEST = lax.Precision.HIGHEST
MESH = pl.DeviceIdType.MESH


def matmul(a, b, contract=((1,), (0,)), precision=None):
    return lax.dot_general(
        a, b, (contract, ((), ())), precision=precision, preferred_element_type=jnp.float32
    )


def hp(a, b, contract=((1,), (0,))):
    return matmul(a, b, contract, HIGHEST)


def kernel(
    n_mem, n_lat,
    prior_hbm, wind_hbm, cell_hbm, value_hbm, prec_hbm, nb_hbm, cnt_hbm,
    out_ref,
    prior, wind, cells, value, prec, nb, cnt, meta, packed, tiles, beside, moved,
    load_sem, halo_send, halo_recv, meta_send, meta_recv, tile_send, tile_recv, back_send, back_recv,
):
    f32, bf16, i32 = jnp.float32, jnp.bfloat16, jnp.int32
    u = lax.axis_index("mem")
    t = lax.axis_index("lat")
    members, _, rows, cols = prior_hbm.shape
    slots = nb_hbm.shape[2]
    n_obs = cell_hbm.shape[1]
    ens = members * n_mem
    big = ens * rows
    half = members * rows

    lat_up, lat_down = lax.rem(t + 1, n_lat), lax.rem(t + n_lat - 1, n_lat)
    mem_up, mem_down = lax.rem(u + 1, n_mem), lax.rem(u + n_mem - 1, n_mem)

    loads = [
        pltpu.make_async_copy(src, dst, load_sem.at[i])
        for i, (src, dst) in enumerate((
            (prior_hbm, prior.at[1]), (wind_hbm, wind.at[1]), (cell_hbm, cells), (value_hbm, value),
            (prec_hbm, prec), (nb_hbm, nb), (cnt_hbm, cnt),
        ))
    ]
    for load in loads:
        load.start()

    barrier = pltpu.get_barrier_semaphore()

    def greet(d, carry):
        for lat in (t, lat_up, lat_down):
            pl.semaphore_signal(
                barrier, inc=1, device_id={"mem": lax.rem(u + d, n_mem), "lat": lat}, device_id_type=MESH
            )
        return carry

    for lat in (lat_up, lat_down):
        pl.semaphore_signal(barrier, inc=1, device_id={"mem": u, "lat": lat}, device_id_type=MESH)
    lax.fori_loop(1, n_mem, greet, 0)
    pl.semaphore_wait(barrier, 3 * n_mem - 1)

    halos = []
    for side, lat in ((0, lat_up), (2, lat_down)):
        for kind, (src, dst) in enumerate(((prior_hbm, prior), (wind_hbm, wind))):
            copy = pltpu.make_async_remote_copy(
                src_ref=src, dst_ref=dst.at[side],
                send_sem=halo_send.at[side // 2, kind], recv_sem=halo_recv.at[side // 2, kind],
                device_id={"mem": u, "lat": lat}, device_id_type=MESH,
            )
            copy.start()
            halos.append(copy)

    for load in loads[2:]:
        load.wait()
    meta[0, 0:1, :] = cells[...].astype(f32)
    meta[0, 1:2, :] = value[...]
    meta[0, 2:3, :] = prec[...]
    meta[0, 3:8, :] = jnp.zeros((5, n_obs), f32)
    metas = []
    for slot, (mem, lat) in enumerate(((u, lat_up), (u, lat_down), (mem_up, t), (mem_down, t))):
        copy = pltpu.make_async_remote_copy(
            src_ref=meta.at[0], dst_ref=meta.at[slot + 1],
            send_sem=meta_send.at[slot], recv_sem=meta_recv.at[slot],
            device_id={"mem": mem, "lat": lat}, device_id_type=MESH,
        )
        copy.start()
        metas.append(copy)

    n_ext = 5 * n_obs
    n_hi = n_ext // W
    listed = jnp.concatenate([nb[r] for r in range(rows)], axis=1)
    counts = jnp.concatenate(
        [jnp.broadcast_to(cnt[r : r + 1, :], (1, slots)) for r in range(rows)], axis=1
    )
    position = lax.broadcasted_iota(i32, (1, rows * slots), 1)
    hi = lax.shift_right_logical(listed, 7)
    lo = lax.bitwise_and(listed, W - 1)
    hi = jnp.where(lax.bitwise_and(position, slots - 1) < counts, hi, n_hi + 8)
    sub = lax.broadcasted_iota(i32, (8 * n_hi, rows * slots), 0)
    owner = position // slots
    key = hi * 8 + owner
    left = (sub == key).astype(f32) + (sub == key + rows).astype(f32)
    right = (lax.broadcasted_iota(i32, (W, rows * slots), 0) == lo).astype(f32)
    member = matmul(left.astype(bf16), right.astype(bf16), ((1,), (1,)))
    member = jnp.concatenate([member[8 * h : 8 * h + 8] for h in range(n_hi)], axis=1)

    for load in loads[:2]:
        load.wait()
    for copy in halos:
        copy.wait()
    wide = 4 * rows
    row_id = lax.broadcasted_iota(i32, (wide, cols), 0)
    col_id = lax.broadcasted_iota(i32, (wide, cols), 1)
    first_row = jnp.where(t == 0, rows, 0)
    last_row = jnp.where(t == n_lat - 1, 2 * rows, 3 * rows)
    inside = (row_id >= first_row) & (row_id < last_row)

    def band(parts):
        return jnp.concatenate(list(parts) + [jnp.zeros((rows, cols), f32)], axis=0)

    east = band(wind[s, 0] for s in range(3))
    north = band(wind[s, 1] for s in range(3))
    east_pos, east_neg = jnp.maximum(east, 0.0), jnp.minimum(east, 0.0)
    north_pos, north_neg = jnp.maximum(north, 0.0), jnp.minimum(north, 0.0)
    fields = []
    for var in range(2):
        kappa = KAPPA[var]
        keep = jnp.where(inside, 1.0 - (east_pos - east_neg + north_pos - north_neg) - 4.0 * kappa, 0.0)
        from_west = jnp.where(inside & (col_id > 0), east_pos + kappa, 0.0)
        from_east = jnp.where(inside & (col_id < cols - 1), kappa - east_neg, 0.0)
        from_south = jnp.where(inside, north_pos + kappa, 0.0)
        from_north = jnp.where(inside, kappa - north_neg, 0.0)
        own = []
        for j in range(members):
            q = jnp.where(inside, band(prior[s, j, var].astype(f32) for s in range(3)), 0.0)
            for _ in range(SECTIONS):
                q = (
                    keep * q
                    + from_west * pltpu.roll(q, 1, 1)
                    + from_east * pltpu.roll(q, cols - 1, 1)
                    + from_south * pltpu.roll(q, 1, 0)
                    + from_north * pltpu.roll(q, wide - 1, 0)
                )
            own.append(q[rows : 2 * rows])
        fields.append(jnp.concatenate(own, axis=0).astype(bf16))
    for k in range(n_mem):
        for place, (var, tile) in enumerate(((0, (k - 1) % n_mem), (0, k), (0, (k + 1) % n_mem), (1, k))):
            packed[k, :, place * W : (place + 1) * W] = fields[var][:, tile * W : (tile + 1) * W]

    def beside_copy(mem, side, lat):
        return pltpu.make_async_remote_copy(
            src_ref=packed.at[mem, :, pl.ds(W, W)], dst_ref=beside.at[side, u],
            send_sem=tile_send.at[1 + side, mem], recv_sem=tile_recv.at[1 + side, u],
            device_id={"mem": mem, "lat": lat}, device_id_type=MESH,
        )

    def tile_copy(mem):
        return pltpu.make_async_remote_copy(
            src_ref=packed.at[mem], dst_ref=tiles.at[u],
            send_sem=tile_send.at[0, mem], recv_sem=tile_recv.at[0, u],
            device_id={"mem": mem, "lat": t}, device_id_type=MESH,
        )

    own_tile = pltpu.make_async_copy(packed.at[u], tiles.at[u], tile_recv.at[0, u])
    own_tile.start()

    def send_tiles(d, carry):
        mem = lax.rem(u + d, n_mem)
        tile_copy(mem).start()
        beside_copy(mem, 0, lat_up).start()
        beside_copy(mem, 1, lat_down).start()
        return carry

    lax.fori_loop(1, n_mem, send_tiles, 0)
    beside_copy(u, 0, lat_up).start()
    beside_copy(u, 1, lat_down).start()

    for copy in metas:
        copy.wait()
    cell = jnp.concatenate([meta[i, 0:1, :] for i in range(5)], axis=1)
    observed = jnp.concatenate([meta[i, 1:2, :] for i in range(5)], axis=1)
    valid = (None, t > 0, t < n_lat - 1, u > 0, u < n_mem - 1)
    precision = jnp.concatenate(
        [meta[0, 2:3, :]] + [jnp.where(valid[i], meta[i, 2:3, :], 0.0) for i in range(1, 5)], axis=1
    )
    cell_row = jnp.floor(cell * (1.0 / W))
    cell_col = cell - W * cell_row

    def spread_out(shifts):
        return jnp.concatenate([jnp.full((1, n_obs), s, f32) for s in shifts], axis=1)

    ext_row = cell_row + spread_out((0.0, -float(rows), float(rows), 0.0, 0.0))
    ext_col = cell_col + spread_out((0.0, 0.0, 0.0, -float(W), float(W)))
    block = lax.bitwise_and(lax.broadcasted_iota(i32, (8, n_ext), 0), rows - 1).astype(f32)
    row_gap = (ext_row - block) * (1.0 / LOC_ROWS)
    col_gap = (ext_col - 0.5 * (W - 1)) * (1.0 / LOC_COLS)
    weight = member * jnp.exp(-0.5 * (row_gap * row_gap + col_gap * col_gap)) * precision
    select = (lax.broadcasted_iota(i32, (W, n_ext), 0).astype(f32) == cell_col).astype(f32).astype(bf16)
    at_row = jnp.where(block == cell_row, 1.0, 0.0)
    ids0 = lax.broadcasted_iota(i32, (big, big), 0)
    ids1 = lax.broadcasted_iota(i32, (big, big), 1)
    same_member = (ids0 // rows == ids1 // rows).astype(f32).astype(bf16)
    same_block = lax.bitwise_and(ids0, rows - 1) == lax.bitwise_and(ids1, rows - 1)
    identity = (ids0 == ids1).astype(f32)

    own_tile.wait()

    def wait_tiles(d, carry):
        mem = lax.rem(u + d, n_mem)
        pltpu.make_async_copy(packed.at[0], tiles.at[mem], tile_recv.at[0, mem]).wait()
        return carry

    def wait_beside(mem, carry):
        for side in range(2):
            pltpu.make_async_copy(
                packed.at[0, :, pl.ds(W, W)], beside.at[side, mem], tile_recv.at[1 + side, mem]
            ).wait()
        return carry

    lax.fori_loop(1, n_mem, wait_tiles, 0)
    lax.fori_loop(0, n_mem, wait_beside, 0)

    states = tiles[...].astype(f32)

    def flat(x):
        return x.reshape(big, x.shape[-1])

    sources = (
        states[:, :, W : 2 * W], beside[0].astype(f32), beside[1].astype(f32),
        states[:, :, 0:W], states[:, :, 2 * W : 3 * W],
    )
    picked = jnp.concatenate(
        [
            matmul(flat(x).astype(bf16), select[:, i * n_obs : (i + 1) * n_obs])
            for i, x in enumerate(sources)
        ],
        axis=1,
    )
    picked = picked.reshape(n_mem, 8, n_ext) * at_row[None]
    obs = matmul(same_member, flat(picked).astype(bf16))
    obs3 = obs.reshape(n_mem, 8, n_ext)
    folded = jnp.sum(obs3, axis=0)
    obs_mean = jnp.sum(folded, axis=0, keepdims=True) * (1.0 / big)
    spread = obs - obs_mean
    innovation = observed - obs_mean
    weighted = flat(spread.reshape(n_mem, 8, n_ext) * weight[None])
    gram = jnp.where(same_block, hp(weighted, spread, ((1,), (1,))), 0.0)
    forcing = jnp.sum(weighted * innovation, axis=1, keepdims=True)

    def fold(x, op):
        folded = op(x.reshape(n_mem, 8, x.shape[-1]), axis=0)
        return folded

    row_sums = jnp.broadcast_to(jnp.sum(jnp.abs(gram), axis=1, keepdims=True), (big, W))
    top = jnp.max(row_sums.reshape(n_mem, 8, W), axis=0)
    top = jnp.maximum(top, pltpu.roll(top, rows, 0))
    bound = (ens - 1.0) + jnp.broadcast_to(top[None], (n_mem, 8, W)).reshape(big, W)[:, 0:1]
    upper = ((ens - 1.0) * identity + gram) / bound
    factor = 1.5 * identity - 0.5 * upper
    lower = factor
    upper = hp(upper, factor)
    for step in range(1, NS_ITERS):
        factor = 1.5 * identity - 0.5 * hp(lower, upper)
        if step < NS_ITERS - 1:
            upper = hp(upper, factor)
        lower = hp(factor, lower)
    root = lower / jnp.sqrt(bound)
    shift = hp(root, hp(root, jnp.broadcast_to(forcing, (big, W))))
    weights = math.sqrt(ens - 1.0) * root + jnp.where(same_block, shift[:, 0:1], 0.0)

    fields3 = jnp.concatenate([states[:, :, W : 2 * W], states[:, :, 3 * W : 4 * W]], axis=2)
    total = jnp.sum(fields3, axis=0)
    centre = (total + pltpu.roll(total, rows, 0)) * (1.0 / ens)
    anomalies = flat(fields3 - centre[None])
    updated = hp(weights, anomalies, ((0,), (0,))).reshape(n_mem, 8, 2 * W) + centre[None]
    for j in range(members):
        for var in range(2):
            moved[:, j, var] = updated[:, j * rows : (j + 1) * rows, var * W : (var + 1) * W].astype(bf16)

    def here(k):
        return out_ref.at[:, :, :, pl.ds(pl.multiple_of(k * W, W), W)]

    def back_copy(mem):
        return pltpu.make_async_remote_copy(
            src_ref=moved.at[mem], dst_ref=here(u),
            send_sem=back_send.at[mem], recv_sem=back_recv.at[u],
            device_id={"mem": mem, "lat": t}, device_id_type=MESH,
        )

    own_back = pltpu.make_async_copy(moved.at[u], here(u), back_recv.at[u])

    def send_back(d, carry):
        back_copy(lax.rem(u + d, n_mem)).start()
        return carry

    lax.fori_loop(1, n_mem, send_back, 0)
    own_back.start()

    def drain(d, carry):
        mem = lax.rem(u + d, n_mem)
        tile_copy(mem).wait_send()
        beside_copy(mem, 0, lat_up).wait_send()
        beside_copy(mem, 1, lat_down).wait_send()
        back_copy(mem).wait_send()
        return carry

    lax.fori_loop(1, n_mem, drain, 0)
    beside_copy(u, 0, lat_up).wait_send()
    beside_copy(u, 1, lat_down).wait_send()
    own_back.wait()

    def wait_back(d, carry):
        mem = lax.rem(u + d, n_mem)
        pltpu.make_async_copy(moved.at[mem], here(mem), back_recv.at[mem]).wait()
        return carry

    lax.fori_loop(1, n_mem, wait_back, 0)


def on_device(n_mem, n_lat, *args):
    prior, wind, cell, value, prec, nb, cnt = args
    members, _, rows, cols = prior.shape
    n_obs = cell.shape[1]
    f32, bf16, i32 = jnp.float32, jnp.bfloat16, jnp.int32
    dma = pltpu.SemaphoreType.DMA
    return pl.pallas_call(
        functools.partial(kernel, n_mem, n_lat),
        out_shape=jax.ShapeDtypeStruct(prior.shape, bf16),
        in_specs=[pl.BlockSpec(memory_space=pl.ANY)] * 7,
        out_specs=pl.BlockSpec(memory_space=pltpu.VMEM),
        scratch_shapes=[
            pltpu.VMEM((3,) + prior.shape, bf16),
            pltpu.VMEM((3,) + wind.shape, f32),
            pltpu.VMEM(cell.shape, i32),
            pltpu.VMEM(value.shape, f32),
            pltpu.VMEM(prec.shape, f32),
            pltpu.VMEM(nb.shape, i32),
            pltpu.VMEM(cnt.shape, i32),
            pltpu.VMEM((5, 8, n_obs), f32),
            pltpu.VMEM((n_mem, members * rows, 4 * W), bf16),
            pltpu.VMEM((n_mem, members * rows, 4 * W), bf16),
            pltpu.VMEM((2, n_mem, members * rows, W), bf16),
            pltpu.VMEM((n_mem, members, 2, rows, W), bf16),
            dma((7,)), dma((2, 2)), dma((2, 2)), dma((4,)), dma((4,)),
            dma((3, n_mem)), dma((3, n_mem)), dma((n_mem,)), dma((n_mem,)),
        ],
        compiler_params=pltpu.CompilerParams(collective_id=0, has_side_effects=True),
    )(prior, wind, cell, value, prec, nb, cnt)


def solution(mesh):
    placed = (
        P("mem", None, "lat", None),
        P(None, "lat", None),
        P("lat", "mem"),
        P("lat", "mem"),
        P("lat", "mem"),
        P("lat", "mem", None),
        P("lat", "mem"),
    )
    return jax.shard_map(
        functools.partial(on_device, mesh.shape["mem"], mesh.shape["lat"]),
        mesh=mesh,
        in_specs=placed,
        out_specs=P("mem", None, "lat", None),
        check_vma=False,
    )
```

time: 94 us -> 28.3 us (0.30); the launches traced: 92.3 us -> 28.1 us
  starting transfers between devices: 32.8 us -> 0 us
  Pallas kernels: 0 us -> 25.4 us
  waiting for transfers between devices: 20.2 us -> 0 us
  local copies, waits for them, and re-layouts: 21 us -> 2.7 us
  blocking collectives: 10.2 us -> 0 us
  matrix products: 5.19 us -> 0 us
  other arithmetic: 2.15 us -> 0 us
    ppermute x12 -> x0, starting transfers between devices: 27 us -> none  [the longest x6 19.2 us: with_halo(): lax.ppermute(tail, axis, [(i, (i + 1) % count) for i in range(ends)])]
    pallas_call x0 -> x1, Pallas kernels: none -> 25.4 us  [on_device(): pl.pallas_call(functools.partial(kernel, n_mem, n_lat), out_shape=jax.Sha...]
    unnamed x28 -> x2, local copies, waits for them, and re-layouts: 16.8 us -> 2.7 us
    ppermute x12 -> x0, waiting for transfers between devices: 13.4 us -> none  [the longest x6 13.3 us: with_halo(): lax.ppermute(head, axis, [((i + 1) % count, i) for i in range(ends)])]
    all_to_all x1 -> x0, blocking collectives: 10.2 us -> none  [on_device(): lax.all_to_all(updated, 'mem', split_axis=0, concat_axis=3, tiled=True)]
    all_to_all x1 -> x0, waiting for transfers between devices: 6.82 us -> none  [on_device(): lax.all_to_all(predict_advance, 'mem', split_axis=3, concat_axis=0, tiled...]
    all_to_all x1 -> x0, starting transfers between devices: 5.83 us -> none  [on_device(): lax.all_to_all(predict_advance, 'mem', split_axis=3, concat_axis=0, tiled...]
    dot_general x22 -> x0, matrix products: 5.19 us -> none  [the longest x1 1.28 us: analyze(): gram_matrix = jnp.einsum('rek,fk->ref', weighted, spread, precision=HIGHEST)]
  transfers between devices with their start and end apart: 13 -> 0, of which waited for: 7 -> 0; matrix products, arithmetic and copies ran while one was open for 10% -> 0% of each run, Pallas kernels for 0% -> 0%
where the time goes in v1:
time: 28.3 us; the launch traced here: 28.1 us
  Pallas kernels  25.4 us (90%)
  local copies, waits for them, and re-layouts  2.7 us (10%)
    pallas_call x1, Pallas kernels, on_device(): pl.pallas_call(functools.partial(kernel, n_mem, n_lat), out_shape=jax.Sha...  25.4 us
    unnamed x2, local copies, waits for them, and re-layouts  2.7 us

profile of v1, /device:TPU:0, one launch (start us, length us, event | category | flops | bytes accessed | tf_op | source)
XLA Modules:
  0.0 28.1 jit_solution(11128888325611114519)
XLA Ops:
  0.0 1.3 %copy.8.cnt_hbm = s32[4,1]{1,0:T(4,128)} copy(s32[4,1]{0,1:T(1,128)} %param.13) | data formatting | bytes 32 | tf_op args[6]
  1.3 25.4 %shard_map.73 = bf16[2,2,4,1024]{3,2,1,0:T(4,128)(2,1)} custom-call(bf16[2,2,4,1024]{3,2,1,0:T(4,128)(2,1)} %prior_hbm.1, f32[2,4,1024]{2,1,0:T(4,128)} %wind_hbm.1, s32[1,256]{1,0:T(1,128)} %cell_hbm.1, f32[1,256]{1,0:T(1,128)} %value_hbm.1, f32[1,256]{1,0:T(1,128)} %prec_hbm.1, s32[4,1,512]{2,1,0:T(1,128)} %nb_hbm.1, s32[4,1]{1,0:T(4,128)} %copy.8.cnt_hbm), custom_call_target="tpu_custom_call" | custom-call | tf_op jit(solution)/shard_map/pallas_call | solution.py:339
  26.7 1.4 %copy.10 = bf16[2,2,4,1024]{3,2,1,0:T(4,128)(2,1)} copy(bf16[2,2,4,1024]{3,2,1,0:T(4,128)(2,1)} %shard_map.73) | data formatting | bytes 65536

commit v2 on v1

--- a/solution.py
+++ b/solution.py
@@ -14,18 +14,24 @@
 LOC_ROWS = 2
 LOC_COLS = 64
 KAPPA = (0.025, 0.0125)
-HIGHEST = lax.Precision.HIGHEST
 MESH = pl.DeviceIdType.MESH
 
 
-def matmul(a, b, contract=((1,), (0,)), precision=None):
-    return lax.dot_general(
-        a, b, (contract, ((), ())), precision=precision, preferred_element_type=jnp.float32
-    )
+def matmul(a, b, contract=((1,), (0,))):
+    return lax.dot_general(a, b, (contract, ((), ())), preferred_element_type=jnp.float32)
+
+
+def halves(x):
+    high = x.astype(jnp.bfloat16)
+    return high, (x - high.astype(jnp.float32)).astype(jnp.bfloat16)
 
 
 def hp(a, b, contract=((1,), (0,))):
-    return matmul(a, b, contract, HIGHEST)
+    a_high, a_low = halves(a)
+    b_high, b_low = halves(b)
+    return matmul(a_high, b_high, contract) + (
+        matmul(a_high, b_low, contract) + matmul(a_low, b_high, contract)
+    )
 
 
 def kernel(
@@ -33,7 +39,7 @@
     prior_hbm, wind_hbm, cell_hbm, value_hbm, prec_hbm, nb_hbm, cnt_hbm,
     out_ref,
     prior, wind, cells, value, prec, nb, cnt, meta, packed, tiles, beside, moved,
-    load_sem, halo_send, halo_recv, meta_send, meta_recv, tile_send, tile_recv, back_send, back_recv,
+    load_sem, halo_send, halo_recv, meta_send, meta_recv, tile_send, tile_recv, back_send, back_recv, ready,
 ):
     f32, bf16, i32 = jnp.float32, jnp.bfloat16, jnp.int32
     u = lax.axis_index("mem")
@@ -45,8 +51,23 @@
     big = ens * rows
     half = members * rows
 
-    lat_up, lat_down = lax.rem(t + 1, n_lat), lax.rem(t + n_lat - 1, n_lat)
-    mem_up, mem_down = lax.rem(u + 1, n_mem), lax.rem(u + n_mem - 1, n_mem)
+    lat_up, lat_down, mem_up, mem_down = t + 1, t - 1, u + 1, u - 1
+    above, below = t < n_lat - 1, t > 0
+    east_of, west_of = u < n_mem - 1, u > 0
+    lats = 1 + above.astype(i32) + below.astype(i32)
+
+    def partner(k):
+        up = k + (k >= u).astype(i32)
+        k = n_mem - 1 - k
+        return jnp.where(2 * u >= n_mem, up, k - (k <= u).astype(i32))
+
+    def signal(sem, mem, lat):
+        pl.semaphore_signal(sem, inc=1, device_id={"mem": mem, "lat": lat}, device_id_type=MESH)
+
+    def signal_lats(sem, mem):
+        signal(sem, mem, t)
+        pl.when(above)(lambda: signal(sem, mem, lat_up))
+        pl.when(below)(lambda: signal(sem, mem, lat_down))
 
     loads = [
         pltpu.make_async_copy(src, dst, load_sem.at[i])
@@ -59,29 +80,39 @@
         load.start()
 
     barrier = pltpu.get_barrier_semaphore()
+    pl.when(above)(lambda: signal(barrier, u, lat_up))
+    pl.when(below)(lambda: signal(barrier, u, lat_down))
 
     def greet(d, carry):
-        for lat in (t, lat_up, lat_down):
-            pl.semaphore_signal(
-                barrier, inc=1, device_id={"mem": lax.rem(u + d, n_mem), "lat": lat}, device_id_type=MESH
-            )
-        return carry
-
-    for lat in (lat_up, lat_down):
-        pl.semaphore_signal(barrier, inc=1, device_id={"mem": u, "lat": lat}, device_id_type=MESH)
-    lax.fori_loop(1, n_mem, greet, 0)
-    pl.semaphore_wait(barrier, 3 * n_mem - 1)
-
-    halos = []
-    for side, lat in ((0, lat_up), (2, lat_down)):
-        for kind, (src, dst) in enumerate(((prior_hbm, prior), (wind_hbm, wind))):
-            copy = pltpu.make_async_remote_copy(
-                src_ref=src, dst_ref=dst.at[side],
-                send_sem=halo_send.at[side // 2, kind], recv_sem=halo_recv.at[side // 2, kind],
+        signal_lats(barrier, n_mem - 1 - d)
+        return carry
+
+    lax.fori_loop(0, n_mem - 1 - u, greet, 0)
+    pl.semaphore_wait(barrier, lats * (u + 1) - 1)
+
+    def halo_copies(side, lat):
+        return [
+            pltpu.make_async_remote_copy(
+                src_ref=src, dst_ref=dst.at[2 * side],
+                send_sem=halo_send.at[side, kind], recv_sem=halo_recv.at[side, kind],
                 device_id={"mem": u, "lat": lat}, device_id_type=MESH,
             )
-            copy.start()
-            halos.append(copy)
+            for kind, (src, dst) in enumerate(((prior_hbm, prior), (wind_hbm, wind)))
+        ]
+
+    def each(copies, act):
+        for copy in copies:
+            getattr(copy, act)()
+
+    up_halo, down_halo = halo_copies(0, lat_up), halo_copies(1, lat_down)
+    pl.when(above)(lambda: each(up_halo, "start"))
+    pl.when(below)(lambda: each(down_halo, "start"))
+
+    def answer(mem, carry):
+        signal_lats(ready, mem)
+        return carry
+
+    lax.fori_loop(0, u, answer, 0)
 
     for load in loads[2:]:
         load.wait()
@@ -89,21 +120,30 @@
     meta[0, 1:2, :] = value[...]
     meta[0, 2:3, :] = prec[...]
     meta[0, 3:8, :] = jnp.zeros((5, n_obs), f32)
-    metas = []
-    for slot, (mem, lat) in enumerate(((u, lat_up), (u, lat_down), (mem_up, t), (mem_down, t))):
-        copy = pltpu.make_async_remote_copy(
+    metas = [
+        pltpu.make_async_remote_copy(
             src_ref=meta.at[0], dst_ref=meta.at[slot + 1],
             send_sem=meta_send.at[slot], recv_sem=meta_recv.at[slot],
             device_id={"mem": mem, "lat": lat}, device_id_type=MESH,
         )
-        copy.start()
-        metas.append(copy)
+        for slot, (mem, lat) in enumerate(((u, lat_up), (u, lat_down), (mem_up, t), (mem_down, t)))
+    ]
+    meta_to = (above, below, east_of, west_of)
+    meta_from = (below, above, west_of, east_of)
+
+    def meta_zero(slot):
+        meta[slot + 1] = jnp.zeros((8, n_obs), f32)
+
+    for slot in (0, 1, 3):
+        pl.when(meta_to[slot])(metas[slot].start)
+    for slot in range(4):
+        pl.when(jnp.logical_not(meta_from[slot]))(functools.partial(meta_zero, slot))
 
     n_ext = 5 * n_obs
     n_hi = n_ext // W
     listed = jnp.concatenate([nb[r] for r in range(rows)], axis=1)
     counts = jnp.concatenate(
-        [jnp.broadcast_to(cnt[r : r + 1, :], (1, slots)) for r in range(rows)], axis=1
+        [jnp.broadcast_to(cnt[:, r : r + 1], (1, slots)) for r in range(rows)], axis=1
     )
     position = lax.broadcasted_iota(i32, (1, rows * slots), 1)
     hi = lax.shift_right_logical(listed, 7)
@@ -119,8 +159,8 @@
 
     for load in loads[:2]:
         load.wait()
-    for copy in halos:
-        copy.wait()
+    pl.when(below)(lambda: each(up_halo, "wait_recv"))
+    pl.when(above)(lambda: each(down_halo, "wait_recv"))
     wide = 4 * rows
     row_id = lax.broadcasted_iota(i32, (wide, cols), 0)
     col_id = lax.broadcasted_iota(i32, (wide, cols), 1)
@@ -174,25 +214,35 @@
             device_id={"mem": mem, "lat": t}, device_id_type=MESH,
         )
 
+    def beside_both(mem, act):
+        pl.when(above)(lambda: getattr(beside_copy(mem, 0, lat_up), act)())
+        pl.when(below)(lambda: getattr(beside_copy(mem, 1, lat_down), act)())
+
+    pl.when(east_of)(lambda: pl.semaphore_wait(ready, lats * (n_mem - 1 - u)))
+    pl.when(east_of)(metas[2].start)
+
+    def send_tiles(k, carry):
+        mem = partner(k)
+        tile_copy(mem).start()
+        beside_both(mem, "start")
+        return carry
+
+    lax.fori_loop(0, n_mem - 1, send_tiles, 0)
+    beside_both(u, "start")
     own_tile = pltpu.make_async_copy(packed.at[u], tiles.at[u], tile_recv.at[0, u])
     own_tile.start()
 
-    def send_tiles(d, carry):
-        mem = lax.rem(u + d, n_mem)
-        tile_copy(mem).start()
-        beside_copy(mem, 0, lat_up).start()
-        beside_copy(mem, 1, lat_down).start()
-        return carry
-
-    lax.fori_loop(1, n_mem, send_tiles, 0)
-    beside_copy(u, 0, lat_up).start()
-    beside_copy(u, 1, lat_down).start()
-
-    for copy in metas:
-        copy.wait()
+    def beside_zero(side):
+        beside[side] = jnp.zeros(beside.shape[1:], bf16)
+
+    pl.when(jnp.logical_not(below))(lambda: beside_zero(0))
+    pl.when(jnp.logical_not(above))(lambda: beside_zero(1))
+
+    for slot in range(4):
+        pl.when(meta_from[slot])(metas[slot].wait_recv)
     cell = jnp.concatenate([meta[i, 0:1, :] for i in range(5)], axis=1)
     observed = jnp.concatenate([meta[i, 1:2, :] for i in range(5)], axis=1)
-    valid = (None, t > 0, t < n_lat - 1, u > 0, u < n_mem - 1)
+    valid = (None,) + meta_from
     precision = jnp.concatenate(
         [meta[0, 2:3, :]] + [jnp.where(valid[i], meta[i, 2:3, :], 0.0) for i in range(1, 5)], axis=1
     )
@@ -218,20 +268,23 @@
 
     own_tile.wait()
 
-    def wait_tiles(d, carry):
-        mem = lax.rem(u + d, n_mem)
+    def wait_tiles(k, carry):
+        mem = partner(k)
         pltpu.make_async_copy(packed.at[0], tiles.at[mem], tile_recv.at[0, mem]).wait()
         return carry
 
-    def wait_beside(mem, carry):
-        for side in range(2):
+    def wait_beside(side):
+        def wait_one(mem, carry):
             pltpu.make_async_copy(
                 packed.at[0, :, pl.ds(W, W)], beside.at[side, mem], tile_recv.at[1 + side, mem]
             ).wait()
-        return carry
-
-    lax.fori_loop(1, n_mem, wait_tiles, 0)
-    lax.fori_loop(0, n_mem, wait_beside, 0)
+            return carry
+
+        lax.fori_loop(0, n_mem, wait_one, 0)
+
+    lax.fori_loop(0, n_mem - 1, wait_tiles, 0)
+    pl.when(below)(lambda: wait_beside(0))
+    pl.when(above)(lambda: wait_beside(1))
 
     states = tiles[...].astype(f32)
 
@@ -260,9 +313,11 @@
     gram = jnp.where(same_block, hp(weighted, spread, ((1,), (1,))), 0.0)
     forcing = jnp.sum(weighted * innovation, axis=1, keepdims=True)
 
-    def fold(x, op):
-        folded = op(x.reshape(n_mem, 8, x.shape[-1]), axis=0)
-        return folded
+    fields3 = jnp.concatenate([states[:, :, W : 2 * W], states[:, :, 3 * W : 4 * W]], axis=2)
+    total = jnp.sum(fields3, axis=0)
+    centre = (total + pltpu.roll(total, rows, 0)) * (1.0 / ens)
+    anomalies = flat(fields3 - centre[None])
+    extra = jnp.concatenate([anomalies, jnp.broadcast_to(forcing, (big, W))], axis=1)
 
     row_sums = jnp.broadcast_to(jnp.sum(jnp.abs(gram), axis=1, keepdims=True), (big, W))
     top = jnp.max(row_sums.reshape(n_mem, 8, W), axis=0)
@@ -276,16 +331,12 @@
         factor = 1.5 * identity - 0.5 * hp(lower, upper)
         if step < NS_ITERS - 1:
             upper = hp(upper, factor)
-        lower = hp(factor, lower)
-    root = lower / jnp.sqrt(bound)
-    shift = hp(root, hp(root, jnp.broadcast_to(forcing, (big, W))))
-    weights = math.sqrt(ens - 1.0) * root + jnp.where(same_block, shift[:, 0:1], 0.0)
-
-    fields3 = jnp.concatenate([states[:, :, W : 2 * W], states[:, :, 3 * W : 4 * W]], axis=2)
-    total = jnp.sum(fields3, axis=0)
-    centre = (total + pltpu.roll(total, rows, 0)) * (1.0 / ens)
-    anomalies = flat(fields3 - centre[None])
-    updated = hp(weights, anomalies, ((0,), (0,))).reshape(n_mem, 8, 2 * W) + centre[None]
+            lower = hp(factor, lower)
+    rooted = hp(factor, hp(lower, extra)) / jnp.sqrt(bound)
+    turned, half_shift = rooted[:, 0 : 2 * W], rooted[:, 2 * W : 2 * W + 1]
+    shift = jnp.sum((turned * half_shift).reshape(n_mem, 8, 2 * W), axis=0)
+    base = centre + shift + pltpu.roll(shift, rows, 0)
+    updated = (math.sqrt(ens - 1.0) * turned).reshape(n_mem, 8, 2 * W) + base[None]
     for j in range(members):
         for var in range(2):
             moved[:, j, var] = updated[:, j * rows : (j + 1) * rows, var * W : (var + 1) * W].astype(bf16)
@@ -302,36 +353,39 @@
 
     own_back = pltpu.make_async_copy(moved.at[u], here(u), back_recv.at[u])
 
-    def send_back(d, carry):
-        back_copy(lax.rem(u + d, n_mem)).start()
-        return carry
-
-    lax.fori_loop(1, n_mem, send_back, 0)
+    def send_back(k, carry):
+        back_copy(partner(k)).start()
+        return carry
+
+    lax.fori_loop(0, n_mem - 1, send_back, 0)
     own_back.start()
 
-    def drain(d, carry):
-        mem = lax.rem(u + d, n_mem)
+    def drain(k, carry):
+        mem = partner(k)
         tile_copy(mem).wait_send()
-        beside_copy(mem, 0, lat_up).wait_send()
-        beside_copy(mem, 1, lat_down).wait_send()
+        beside_both(mem, "wait_send")
+        return carry
+
+    lax.fori_loop(0, n_mem - 1, drain, 0)
+    beside_both(u, "wait_send")
+    pl.when(above)(lambda: each(up_halo, "wait_send"))
+    pl.when(below)(lambda: each(down_halo, "wait_send"))
+    for slot in range(4):
+        pl.when(meta_to[slot])(metas[slot].wait_send)
+    own_back.wait()
+
+    def wait_back(k, carry):
+        mem = partner(k)
         back_copy(mem).wait_send()
-        return carry
-
-    lax.fori_loop(1, n_mem, drain, 0)
-    beside_copy(u, 0, lat_up).wait_send()
-    beside_copy(u, 1, lat_down).wait_send()
-    own_back.wait()
-
-    def wait_back(d, carry):
-        mem = lax.rem(u + d, n_mem)
         pltpu.make_async_copy(moved.at[mem], here(mem), back_recv.at[mem]).wait()
         return carry
 
-    lax.fori_loop(1, n_mem, wait_back, 0)
+    lax.fori_loop(0, n_mem - 1, wait_back, 0)
 
 
 def on_device(n_mem, n_lat, *args):
     prior, wind, cell, value, prec, nb, cnt = args
+    cnt = cnt.T
     members, _, rows, cols = prior.shape
     n_obs = cell.shape[1]
     f32, bf16, i32 = jnp.float32, jnp.bfloat16, jnp.int32
@@ -355,7 +409,7 @@
             pltpu.VMEM((2, n_mem, members * rows, W), bf16),
             pltpu.VMEM((n_mem, members, 2, rows, W), bf16),
             dma((7,)), dma((2, 2)), dma((2, 2)), dma((4,)), dma((4,)),
-            dma((3, n_mem)), dma((3, n_mem)), dma((n_mem,)), dma((n_mem,)),
+            dma((3, n_mem)), dma((3, n_mem)), dma((n_mem,)), dma((n_mem,)), pltpu.SemaphoreType.REGULAR,
         ],
         compiler_params=pltpu.CompilerParams(collective_id=0, has_side_effects=True),
     )(prior, wind, cell, value, prec, nb, cnt)

time: 28.3 us -> 21.8 us (0.77)
  Pallas kernels: 25.4 us -> 20.2 us
  local copies, waits for them, and re-layouts: 2.7 us -> 1.39 us
    pallas_call x1, Pallas kernels: 25.4 us -> 20.2 us  [on_device(): pl.pallas_call(functools.partial(kernel, n_mem, n_lat), out_shape=jax.Sha...]
    unnamed x2 -> x1, local copies, waits for them, and re-layouts: 2.7 us -> 1.39 us
where the time goes in v2:
time: 21.8 us; the launch traced here: 21.6 us
  Pallas kernels  20.2 us (93%)
  local copies, waits for them, and re-layouts  1.39 us (6%)
    pallas_call x1, Pallas kernels, on_device(): pl.pallas_call(functools.partial(kernel, n_mem, n_lat), out_shape=jax.Sha...  20.2 us
    unnamed x1, local copies, waits for them, and re-layouts  1.39 us

profile of v2, /device:TPU:0, one launch (start us, length us, event | category | flops | bytes accessed | tf_op | source)
XLA Modules:
  0.0 21.6 jit_solution(3543123679370021851)
XLA Ops:
  0.0 20.2 %shard_map.73 = bf16[2,2,4,1024]{3,2,1,0:T(4,128)(2,1)} custom-call(bf16[2,2,4,1024]{3,2,1,0:T(4,128)(2,1)} %prior_hbm.1, f32[2,4,1024]{2,1,0:T(4,128)} %wind_hbm.1, s32[1,256]{1,0:T(1,128)} %cell_hbm.1, f32[1,256]{1,0:T(1,128)} %value_hbm.1, f32[1,256]{1,0:T(1,128)} %prec_hbm.1, s32[4,1,512]{2,1,0:T(1,128)} %nb_hbm.1, s32[1,4]{1,0:T(1,128)} %bitcast.1), custom_call_target="tpu_custom_call" | custom-call | tf_op jit(solution)/shard_map/pallas_call | solution.py:393
  20.2 1.4 %copy.9 = bf16[2,2,4,1024]{3,2,1,0:T(4,128)(2,1)} copy(bf16[2,2,4,1024]{3,2,1,0:T(4,128)(2,1)} %shard_map.73) | data formatting | bytes 65536

commit v3 on v2

--- a/solution.py
+++ b/solution.py
@@ -392,7 +392,7 @@
     dma = pltpu.SemaphoreType.DMA
     return pl.pallas_call(
         functools.partial(kernel, n_mem, n_lat),
-        out_shape=jax.ShapeDtypeStruct(prior.shape, bf16),
+        out_shape=pltpu.VMEM(prior.shape, bf16),
         in_specs=[pl.BlockSpec(memory_space=pl.ANY)] * 7,
         out_specs=pl.BlockSpec(memory_space=pltpu.VMEM),
         scratch_shapes=[

time: 21.8 us -> 20.4 us (0.936)
  local copies, waits for them, and re-layouts: 1.39 us -> 0.62 us
  Pallas kernels: 20.2 us -> 19.6 us
    unnamed x1, local copies, waits for them, and re-layouts: 1.39 us -> 0.62 us
    pallas_call x1, Pallas kernels: 20.2 us -> 19.6 us  [on_device(): pl.pallas_call(functools.partial(kernel, n_mem, n_lat), out_shape=pltpu.V...]
where the time goes in v3:
time: 20.4 us; the launch traced here: 20.2 us
  Pallas kernels  19.6 us (96%)
  local copies, waits for them, and re-layouts  0.62 us (3%)
    pallas_call x1, Pallas kernels, on_device(): pl.pallas_call(functools.partial(kernel, n_mem, n_lat), out_shape=pltpu.V...  19.6 us
    unnamed x1, local copies, waits for them, and re-layouts  0.62 us

profile of v3, /device:TPU:0, one launch (start us, length us, event | category | flops | bytes accessed | tf_op | source)
XLA Modules:
  0.0 20.2 jit_solution(12375805671080074159)
XLA Ops:
  0.0 19.6 %shard_map.73 = bf16[2,2,4,1024]{3,2,1,0:T(4,128)(2,1)S(1)} custom-call(bf16[2,2,4,1024]{3,2,1,0:T(4,128)(2,1)} %prior_hbm.1, f32[2,4,1024]{2,1,0:T(4,128)} %wind_hbm.1, s32[1,256]{1,0:T(1,128)} %cell_hbm.1, f32[1,256]{1,0:T(1,128)} %value_hbm.1, f32[1,256]{1,0:T(1,128)} %prec_hbm.1, s32[4,1,512]{2,1,0:T(1,128)} %nb_hbm.1, s32[1,4]{1,0:T(1,128)} %bitcast.1), custom_call_target="tpu_custom_call" | custom-call | tf_op jit(solution)/shard_map/pallas_call | solution.py:393
  19.6 0.6 %copy.9 = bf16[2,2,4,1024]{3,2,1,0:T(4,128)(2,1)} copy(bf16[2,2,4,1024]{3,2,1,0:T(4,128)(2,1)S(1)} %shard_map.73) | data formatting | bytes 65536

commit v4 on v3

--- a/solution.py
+++ b/solution.py
@@ -89,6 +89,8 @@
 
     lax.fori_loop(0, n_mem - 1 - u, greet, 0)
     pl.semaphore_wait(barrier, lats * (u + 1) - 1)
+    for load in loads[:2]:
+        load.wait()
 
     def halo_copies(side, lat):
         return [
@@ -97,7 +99,7 @@
                 send_sem=halo_send.at[side, kind], recv_sem=halo_recv.at[side, kind],
                 device_id={"mem": u, "lat": lat}, device_id_type=MESH,
             )
-            for kind, (src, dst) in enumerate(((prior_hbm, prior), (wind_hbm, wind)))
+            for kind, (src, dst) in enumerate(((prior.at[1], prior), (wind.at[1], wind)))
         ]
 
     def each(copies, act):
@@ -157,8 +159,6 @@
     member = matmul(left.astype(bf16), right.astype(bf16), ((1,), (1,)))
     member = jnp.concatenate([member[8 * h : 8 * h + 8] for h in range(n_hi)], axis=1)
 
-    for load in loads[:2]:
-        load.wait()
     pl.when(below)(lambda: each(up_halo, "wait_recv"))
     pl.when(above)(lambda: each(down_halo, "wait_recv"))
     wide = 4 * rows

time: 20.4 us -> 20.1 us (0.985)
  Pallas kernels: 19.6 us -> 19.3 us
    pallas_call x1, Pallas kernels: 19.6 us -> 19.3 us  [on_device(): pl.pallas_call(functools.partial(kernel, n_mem, n_lat), out_shape=pltpu.V...]
where the time goes in v4:
time: 20.1 us; the launch traced here: 19.9 us
  Pallas kernels  19.3 us (96%)
  local copies, waits for them, and re-layouts  0.62 us (3%)
    pallas_call x1, Pallas kernels, on_device(): pl.pallas_call(functools.partial(kernel, n_mem, n_lat), out_shape=pltpu.V...  19.3 us
    unnamed x1, local copies, waits for them, and re-layouts  0.62 us

profile of v4, /device:TPU:0, one launch (start us, length us, event | category | flops | bytes accessed | tf_op | source)
XLA Modules:
  0.0 19.9 jit_solution(371431273170490593)
XLA Ops:
  0.0 19.3 %shard_map.73 = bf16[2,2,4,1024]{3,2,1,0:T(4,128)(2,1)S(1)} custom-call(bf16[2,2,4,1024]{3,2,1,0:T(4,128)(2,1)} %prior_hbm.1, f32[2,4,1024]{2,1,0:T(4,128)} %wind_hbm.1, s32[1,256]{1,0:T(1,128)} %cell_hbm.1, f32[1,256]{1,0:T(1,128)} %value_hbm.1, f32[1,256]{1,0:T(1,128)} %prec_hbm.1, s32[4,1,512]{2,1,0:T(1,128)} %nb_hbm.1, s32[1,4]{1,0:T(1,128)} %bitcast.1), custom_call_target="tpu_custom_call" | custom-call | tf_op jit(solution)/shard_map/pallas_call | solution.py:393
  19.3 0.6 %copy.9 = bf16[2,2,4,1024]{3,2,1,0:T(4,128)(2,1)} copy(bf16[2,2,4,1024]{3,2,1,0:T(4,128)(2,1)S(1)} %shard_map.73) | data formatting | bytes 65536
